TPU v7x, 256 devices: a whole 4x4x8 slice. The times are simulated.
256 devices in a mesh: gx: 8 (over y, core), gy: 4 (over z_lo), gz: 8 (over z_hi, x).
Axes of the slice: x: 4, y: 4, z: 8 (z_hi: 2, z_lo: 4; z = z_hi * 4 + z_lo), core: 2. Of those that a mesh axis runs over, the one named last changes fastest.
Arguments:
- tokens: bfloat16 [2048, 8192], P(('gx', 'gy'), 'gz'), may hold values from -6 to 6
- gate_weight: bfloat16 [8192, 28672], P('gz', ('gx', 'gy')), may hold values from -0.0625 to 0.0625
- up_weight: bfloat16 [8192, 28672], P('gz', ('gx', 'gy')), may hold values from -0.0625 to 0.0625
- down_weight: bfloat16 [28672, 8192], P(('gx', 'gy'), 'gz'), may hold values from -0.03125 to 0.03125
Outputs:
- layer_output: bfloat16 [2048, 8192], P(('gx', 'gy'), 'gz')
All inputs are finite; a program needn't handle non-finite values.
Results may differ from a plain program's by a relative error of at most 0.029.
Values may be sent and summed in bfloat16 or wider, within the bound.
A program may use at most 128 MiB of HBM per device.

v0:
```python
import jax
import jax.numpy as jnp
from jax import lax
from jax.sharding import PartitionSpec as P


def shards(tokens, gate_weight, up_weight, down_weight):
    gathered = lax.all_gather(tokens, "gx", axis=0, tiled=True)

    def column_product(weight_piece):
        return jnp.dot(gathered, weight_piece, preferred_element_type=jnp.float32)

    gate_partial = column_product(lax.all_gather(gate_weight, "gy", axis=1, tiled=True))
    up_partial = column_product(lax.all_gather(up_weight, "gy", axis=1, tiled=True))
    gate_sum, up_sum = (
        lax.psum_scatter(
            gate_partial.astype(jnp.bfloat16), "gz", scatter_dimension=0, tiled=True
        ).astype(jnp.float32),
        lax.psum_scatter(
            up_partial.astype(jnp.bfloat16), "gz", scatter_dimension=0, tiled=True
        ).astype(jnp.float32),
    )
    local_hidden = (jax.nn.silu(gate_sum) * up_sum).astype(jnp.bfloat16)
    hidden = lax.all_gather(local_hidden, "gz", axis=0, tiled=True)
    down_partial = jnp.dot(
        hidden,
        lax.all_gather(down_weight, "gy", axis=0, tiled=True),
        preferred_element_type=jnp.float32,
    )
    layer_output = lax.psum_scatter(
        down_partial.astype(jnp.bfloat16), "gx", scatter_dimension=0, tiled=True
    )
    return layer_output


def solution(mesh):
    return jax.shard_map(
        shards,
        mesh=mesh,
        in_specs=(
            P(("gx", "gy"), "gz"),
            P("gz", ("gx", "gy")),
            P("gz", ("gx", "gy")),
            P(("gx", "gy"), "gz"),
        ),
        out_specs=P(("gx", "gy"), "gz"),
        check_vma=False,
    )
```

profile of v0, /device:TPU:2, one launch (start us, length us, event | category | flops | bytes accessed | tf_op | source)
XLA Modules:
  0.0 839.3 jit_solution(120754620333667691)
XLA Ops:
  6.5 0.0 all-gather.6.cloned.1.call-start
  6.5 0.7 all-gather.6.cloned.1.call-update
  7.3 0.0 all-gather.8.cloned.1.call-start
  7.3 0.7 all-gather.8.cloned.1.call-update
  8.0 0.0 all-gather.10.cloned.1.call-start
  8.1 0.7 all-gather.10.cloned.1.call-update
  8.7 0.0 reduce-scatter.4.cloned.1.call-start
  8.8 29.3 %all-gather.6.cloned.1.call-done = bf16[512,1024]{1,0:T(8,128)(2,1)} async-done(((bf16[64,1024]{1,0:T(8,128)(2,1)}), bf16[512,1024]{1,0:T(8,128)(2,1)}) %all-gather.6.cloned.1.call-update) | async-done | bytes 1048592 | tf_op jit(solution)/shard_map/all_gather | solution.py:8
  38.1 0.0 copy-start
  38.1 137.6 %all-gather.8.cloned.1.call-done = bf16[1024,3584]{1,0:T(8,128)(2,1)} async-done(((bf16[1024,896]{1,0:T(8,128)(2,1)}), bf16[1024,3584]{1,0:T(8,128)(2,1)}) %all-gather.8.cloned.1.call-update) | async-done | bytes 7340048 | tf_op jit(solution)/shard_map/all_gather | solution.py:13
  175.7 9.2 %convolution_convert_fusion.1 = bf16[512,3584]{1,0:T(8,128)(2,1)} fusion(bf16[512,1024]{1,0:T(8,128)(2,1)} %all-gather.6.cloned.1.call-done, bf16[1024,3584]{1,0:T(8,128)(2,1)} %all-gather.8.cloned.1.call-done), kind=kOutput, calls=%fused_computation.1 | convolution fusion | flops 3759931392 | bytes 12058624 | tf_op jit(solution)/shard_map/dot_general | solution.py:11
  184.9 0.0 reduce-scatter.4.cloned.1.call-update
  184.9 0.0 reduce-scatter.6.cloned.1.call-start
  185.0 128.1 %all-gather.10.cloned.1.call-done = bf16[1024,3584]{1,0:T(8,128)(2,1)} async-done(((bf16[1024,896]{1,0:T(8,128)(2,1)}), bf16[1024,3584]{1,0:T(8,128)(2,1)}) %all-gather.10.cloned.1.call-update) | async-done | bytes 7340048 | tf_op jit(solution)/shard_map/all_gather | solution.py:14
  313.1 0.0 copy-done
  313.1 8.4 %convolution_convert_fusion = bf16[512,3584]{1,0:T(8,128)(2,1)} fusion(bf16[512,1024]{1,0:T(8,128)(2,1)S(1)} %copy-done, bf16[1024,3584]{1,0:T(8,128)(2,1)} %all-gather.10.cloned.1.call-done), kind=kOutput, calls=%fused_computation | convolution fusion | flops 3759931392 | bytes 12058624 | tf_op jit(solution)/shard_map/dot_general | solution.py:11
  321.5 0.0 reduce-scatter.6.cloned.1.call-update
  321.6 0.0 all-gather.14.cloned.1.call-start
  321.6 0.5 all-gather.14.cloned.1.call-update
  322.1 0.0 all-gather.12.cloned.1.call-start
  322.2 115.4 %reduce-scatter.4.cloned.1.call-done = bf16[64,3584]{1,0:T(8,128)(2,1)} async-done(((bf16[512,3584]{1,0:T(8,128)(2,1)}), bf16[64,3584]{1,0:T(8,128)(2,1)}) %reduce-scatter.4.cloned.1.call-update) | async-done | bytes 458768 | tf_op jit(solution)/shard_map/reduce_scatter | solution.py:16
  437.6 121.3 %reduce-scatter.6.cloned.1.call-done = bf16[64,3584]{1,0:T(8,128)(2,1)} async-done(((bf16[512,3584]{1,0:T(8,128)(2,1)}), bf16[64,3584]{1,0:T(8,128)(2,1)}) %reduce-scatter.6.cloned.1.call-update) | async-done | bytes 458768 | tf_op jit(solution)/shard_map/reduce_scatter | solution.py:19
  558.9 2.2 fusion.4
  561.1 0.0 all-gather.12.cloned.1.call-update
  561.1 0.0 reduce-scatter.8.cloned.1.call-start
  561.2 131.1 %all-gather.14.cloned.1.call-done = bf16[3584,1024]{1,0:T(8,128)(2,1)} async-done(((bf16[896,1024]{1,0:T(8,128)(2,1)}), bf16[3584,1024]{1,0:T(8,128)(2,1)}) %all-gather.14.cloned.1.call-update) | async-done | bytes 7340048 | tf_op jit(solution)/shard_map/all_gather | solution.py:27
  692.3 100.6 %all-gather.12.cloned.1.call-done = bf16[512,3584]{1,0:T(8,128)(2,1)} async-done(((bf16[64,3584]{1,0:T(8,128)(2,1)}), bf16[512,3584]{1,0:T(8,128)(2,1)}) %all-gather.12.cloned.1.call-update) | async-done | bytes 3670032 | tf_op jit(solution)/shard_map/all_gather | solution.py:24
  792.9 9.1 %convolution_convert_fusion.2 = bf16[512,1024]{1,0:T(8,128)(2,1)} fusion(bf16[512,3584]{1,0:T(8,128)(2,1)} %all-gather.12.cloned.1.call-done, bf16[3584,1024]{1,0:T(8,128)(2,1)} %all-gather.14.cloned.1.call-done), kind=kOutput, calls=%fused_computation.2 | convolution fusion | flops 3758620672 | bytes 12058624 | tf_op jit(solution)/shard_map/dot_general | solution.py:25
  802.0 0.0 reduce-scatter.8.cloned.1.call-update
  802.0 30.5 %reduce-scatter.8.cloned.1.call-done = bf16[64,1024]{1,0:T(8,128)(2,1)} async-done(((bf16[512,1024]{1,0:T(8,128)(2,1)}), bf16[64,1024]{1,0:T(8,128)(2,1)}) %reduce-scatter.8.cloned.1.call-update) | async-done | bytes 131088 | tf_op jit(solution)/shard_map/reduce_scatter | solution.py:30
Async XLA Ops:
  6.5 31.6 %all-gather.6.cloned.1.call-start = ((), (), s32[]{:S(2)}) async-start(), calls=%async_computation.3 | async-start | bytes 1179648 | tf_op jit(solution)/shard_map/all_gather | solution.py:8
  7.3 168.4 %all-gather.8.cloned.1.call-start = ((), (), s32[]{:S(2)}) async-start(), calls=%async_computation.4 | async-start | bytes 9175040 | tf_op jit(solution)/shard_map/all_gather | solution.py:13
  8.0 305.1 %all-gather.10.cloned.1.call-start = ((), (), s32[]{:S(2)}) async-start(), calls=%async_computation.6 | async-start | bytes 9175040 | tf_op jit(solution)/shard_map/all_gather | solution.py:14
  8.7 428.9 %reduce-scatter.4.cloned.1.call-start = ((), (), s32[]{:S(2)}) async-start(), calls=%async_computation.5 | async-start | bytes 4128768 | tf_op jit(solution)/shard_map/reduce_scatter | solution.py:16
  38.1 275.0 %copy-start = (bf16[512,1024]{1,0:T(8,128)(2,1)S(1)}, bf16[512,1024]{1,0:T(8,128)(2,1)}, u32[]{:S(2)}) copy-start(bf16[512,1024]{1,0:T(8,128)(2,1)} %all-gather.6.cloned.1.call-done) | copy-start | bytes 3145732
  184.9 374.0 %reduce-scatter.6.cloned.1.call-start = ((), (), s32[]{:S(2)}) async-start(), calls=%async_computation.7 | async-start | bytes 4128768 | tf_op jit(solution)/shard_map/reduce_scatter | solution.py:19
  321.6 370.7 %all-gather.14.cloned.1.call-start = ((), (), s32[]{:S(2)}) async-start(), calls=%async_computation.9 | async-start | bytes 9175040 | tf_op jit(solution)/shard_map/all_gather | solution.py:27
  322.1 470.7 %all-gather.12.cloned.1.call-start = ((), (), s32[]{:S(2)}) async-start(), calls=%async_computation.8 | async-start | bytes 4128768 | tf_op jit(solution)/shard_map/all_gather | solution.py:24
  561.1 271.4 %reduce-scatter.8.cloned.1.call-start = ((), (), s32[]{:S(2)}) async-start(), calls=%async_computation.10 | async-start | bytes 1179648 | tf_op jit(solution)/shard_map/reduce_scatter | solution.py:30
Sparse Core Ops, SparseCore 0:
  9.2 28.8 all-gather.5
  40.0 135.6 all-gather.7
  177.5 135.5 all-gather.9
  317.2 120.3 reduce-scatter.3
  442.3 116.5 reduce-scatter.5
  560.6 131.6 all-gather.13
  694.9 97.9 all-gather.11
  802.1 30.3 reduce-scatter.7
where the time goes:
time: 839 us
  waiting for transfers between devices  797 us (95%)
  matrix products  26.8 us (3%)
  between operations  13.5 us (2%)
    all_gather x1, waiting for transfers between devices, shards(): lax.all_gather(gate_weight, 'gy', axis=1, tiled=True)  138 us
    all_gather x1, waiting for transfers between devices, shards(): lax.all_gather(down_weight, 'gy', axis=0, tiled=True)  131 us
    all_gather x1, waiting for transfers between devices, shards(): lax.all_gather(up_weight, 'gy', axis=1, tiled=True)  128 us
    reduce_scatter x1, waiting for transfers between devices, shards(): lax.psum_scatter(up_partial.astype(jnp.bfloat16), 'gz', scatter_dimension...  121 us
    reduce_scatter x1, waiting for transfers between devices, shards(): lax.psum_scatter(gate_partial.astype(jnp.bfloat16), 'gz', scatter_dimensi...  115 us
    all_gather x1, waiting for transfers between devices, shards(): hidden = lax.all_gather(local_hidden, 'gz', axis=0, tiled=True)  101 us
    reduce_scatter x1, waiting for transfers between devices, shards(): lax.psum_scatter(down_partial.astype(jnp.bfloat16), 'gx', scatter_dimensi...  30.5 us
    all_gather x1, waiting for transfers between devices, shards(): gathered = lax.all_gather(tokens, 'gx', axis=0, tiled=True)  29.3 us
  transfers between devices with their start and end apart: 8, of which 8 were waited for; matrix products, arithmetic and copies ran while one was open for 2% of the time, Pallas kernels for 0%

commit v1 on v0

--- a/solution.py
+++ b/solution.py
@@ -5,7 +5,11 @@
 
 
 def shards(tokens, gate_weight, up_weight, down_weight):
-    gathered = lax.all_gather(tokens, "gx", axis=0, tiled=True)
+    length = lax.axis_size("gx")
+    repeats = [length if d == 0 else 1 for d in range(tokens.ndim)]
+    gathered = lax.all_to_all(
+        jnp.tile(tokens, repeats), "gx", split_axis=0, concat_axis=0, tiled=True
+    )
 
     def column_product(weight_piece):
         return jnp.dot(gathered, weight_piece, preferred_element_type=jnp.float32)

time: 839 us -> 810 us (0.965)
  waiting for transfers between devices: 797 us -> 746 us
  blocking collectives: 0 us -> 20.4 us
    all_gather x1 -> x0, waiting for transfers between devices: 29.3 us -> none  [shards(): gathered = lax.all_gather(tokens, 'gx', axis=0, tiled=True)]
    all_to_all x0 -> x1, blocking collectives: none -> 20.4 us  [shards(): lax.all_to_all(jnp.tile(tokens, repeats), 'gx', split_axis=0, concat_axis...]
    all_gather x1, waiting for transfers between devices: 138 us -> 119 us  [shards(): lax.all_gather(gate_weight, 'gy', axis=1, tiled=True)]
  transfers between devices with their start and end apart: 8 -> 7, of which waited for: 8 -> 7; matrix products, arithmetic and copies ran while one was open for 2% -> 2% of each run, Pallas kernels for 0% -> 0%
where the time goes in v1:
time: 810 us
  waiting for transfers between devices  746 us (92%)
  matrix products  26.1 us (3%)
  blocking collectives  20.4 us (3%)
  between operations  13.5 us (2%)
    all_gather x1, waiting for transfers between devices, shards(): lax.all_gather(down_weight, 'gy', axis=0, tiled=True)  131 us
    all_gather x1, waiting for transfers between devices, shards(): lax.all_gather(up_weight, 'gy', axis=1, tiled=True)  129 us
    reduce_scatter x1, waiting for transfers between devices, shards(): lax.psum_scatter(up_partial.astype(jnp.bfloat16), 'gz', scatter_dimension...  119 us
    all_gather x1, waiting for transfers between devices, shards(): lax.all_gather(gate_weight, 'gy', axis=1, tiled=True)  119 us
    reduce_scatter x1, waiting for transfers between devices, shards(): lax.psum_scatter(gate_partial.astype(jnp.bfloat16), 'gz', scatter_dimensi...  116 us
    all_gather x1, waiting for transfers between devices, shards(): hidden = lax.all_gather(local_hidden, 'gz', axis=0, tiled=True)  100 us
    reduce_scatter x1, waiting for transfers between devices, shards(): lax.psum_scatter(down_partial.astype(jnp.bfloat16), 'gx', scatter_dimensi...  30.5 us
    all_to_all x1, blocking collectives, shards(): lax.all_to_all(jnp.tile(tokens, repeats), 'gx', split_axis=0, concat_axis...  20.4 us
  transfers between devices with their start and end apart: 7, of which 7 were waited for; matrix products, arithmetic and copies ran while one was open for 2% of the time, Pallas kernels for 0%

profile of v1, /device:TPU:2, one launch (start us, length us, event | category | flops | bytes accessed | tf_op | source)
XLA Modules:
  0.0 809.8 jit_solution(7448881920751002648)
XLA Ops:
  6.5 0.0 all-gather.5.cloned.1.call-start
  6.5 0.7 all-gather.5.cloned.1.call-update
  7.3 0.0 all-gather.7.cloned.1.call-start
  7.3 0.7 all-gather.7.cloned.1.call-update
  8.0 0.0 reduce-scatter.4.cloned.1.call-start
  8.1 1.0 tile.2
  9.1 20.4 %all_to_all.9 = bf16[8,64,1024]{2,1,0:T(8,128)(2,1)S(1)} all-to-all(bf16[8,64,1024]{2,1,0:T(8,128)(2,1)S(1)} %tile.2), channel_id=1, replica_groups=mesh['gx'=8,'gy'=4,'gz'=8] {'gx'}, dimensions={0} | all-to-all | bytes 2097152 | tf_op jit(solution)/shard_map/all_to_all | solution.py:10
  29.4 118.5 %all-gather.5.cloned.1.call-done = bf16[1024,3584]{1,0:T(8,128)(2,1)} async-done(((bf16[1024,896]{1,0:T(8,128)(2,1)}), bf16[1024,3584]{1,0:T(8,128)(2,1)}) %all-gather.5.cloned.1.call-update) | async-done | bytes 7340048 | tf_op jit(solution)/shard_map/all_gather | solution.py:17
  148.0 8.5 %convolution_convert_fusion.1 = bf16[512,3584]{1,0:T(8,128)(2,1)} fusion(bf16[512,1024]{1,0:T(8,128)(2,1)S(1)} %bitcast.7, bf16[1024,3584]{1,0:T(8,128)(2,1)} %all-gather.5.cloned.1.call-done), kind=kOutput, calls=%fused_computation.1 | convolution fusion | flops 3759931392 | bytes 12058624 | tf_op jit(solution)/shard_map/dot_general | solution.py:15
  156.5 0.0 reduce-scatter.4.cloned.1.call-update
  156.5 0.0 reduce-scatter.6.cloned.1.call-start
  156.6 128.8 %all-gather.7.cloned.1.call-done = bf16[1024,3584]{1,0:T(8,128)(2,1)} async-done(((bf16[1024,896]{1,0:T(8,128)(2,1)}), bf16[1024,3584]{1,0:T(8,128)(2,1)}) %all-gather.7.cloned.1.call-update) | async-done | bytes 7340048 | tf_op jit(solution)/shard_map/all_gather | solution.py:18
  285.4 8.5 %convolution_convert_fusion = bf16[512,3584]{1,0:T(8,128)(2,1)} fusion(bf16[512,1024]{1,0:T(8,128)(2,1)S(1)} %bitcast.8, bf16[1024,3584]{1,0:T(8,128)(2,1)} %all-gather.7.cloned.1.call-done), kind=kOutput, calls=%fused_computation | convolution fusion | flops 3759931392 | bytes 12058624 | tf_op jit(solution)/shard_map/dot_general | solution.py:15
  293.8 0.0 reduce-scatter.6.cloned.1.call-update
  293.9 0.0 all-gather.11.cloned.1.call-start
  293.9 0.5 all-gather.11.cloned.1.call-update
  294.5 0.0 all-gather.9.cloned.1.call-start
  294.5 115.6 %reduce-scatter.4.cloned.1.call-done = bf16[64,3584]{1,0:T(8,128)(2,1)} async-done(((bf16[512,3584]{1,0:T(8,128)(2,1)}), bf16[64,3584]{1,0:T(8,128)(2,1)}) %reduce-scatter.4.cloned.1.call-update) | async-done | bytes 458768 | tf_op jit(solution)/shard_map/reduce_scatter | solution.py:20
  410.1 119.4 %reduce-scatter.6.cloned.1.call-done = bf16[64,3584]{1,0:T(8,128)(2,1)} async-done(((bf16[512,3584]{1,0:T(8,128)(2,1)}), bf16[64,3584]{1,0:T(8,128)(2,1)}) %reduce-scatter.6.cloned.1.call-update) | async-done | bytes 458768 | tf_op jit(solution)/shard_map/reduce_scatter | solution.py:23
  529.5 2.2 fusion.4
  531.7 0.0 all-gather.9.cloned.1.call-update
  531.7 0.0 reduce-scatter.8.cloned.1.call-start
  531.8 131.0 %all-gather.11.cloned.1.call-done = bf16[3584,1024]{1,0:T(8,128)(2,1)} async-done(((bf16[896,1024]{1,0:T(8,128)(2,1)}), bf16[3584,1024]{1,0:T(8,128)(2,1)}) %all-gather.11.cloned.1.call-update) | async-done | bytes 7340048 | tf_op jit(solution)/shard_map/all_gather | solution.py:31
  662.8 100.5 %all-gather.9.cloned.1.call-done = bf16[512,3584]{1,0:T(8,128)(2,1)} async-done(((bf16[64,3584]{1,0:T(8,128)(2,1)}), bf16[512,3584]{1,0:T(8,128)(2,1)}) %all-gather.9.cloned.1.call-update) | async-done | bytes 3670032 | tf_op jit(solution)/shard_map/all_gather | solution.py:28
  763.3 9.1 %convolution_convert_fusion.2 = bf16[512,1024]{1,0:T(8,128)(2,1)} fusion(bf16[512,3584]{1,0:T(8,128)(2,1)} %all-gather.9.cloned.1.call-done, bf16[3584,1024]{1,0:T(8,128)(2,1)} %all-gather.11.cloned.1.call-done), kind=kOutput, calls=%fused_computation.2 | convolution fusion | flops 3758620672 | bytes 12058624 | tf_op jit(solution)/shard_map/dot_general | solution.py:29
  772.4 0.0 reduce-scatter.8.cloned.1.call-update
  772.4 30.5 %reduce-scatter.8.cloned.1.call-done = bf16[64,1024]{1,0:T(8,128)(2,1)} async-done(((bf16[512,1024]{1,0:T(8,128)(2,1)}), bf16[64,1024]{1,0:T(8,128)(2,1)}) %reduce-scatter.8.cloned.1.call-update) | async-done | bytes 131088 | tf_op jit(solution)/shard_map/reduce_scatter | solution.py:34
Async XLA Ops:
  6.5 141.5 %all-gather.5.cloned.1.call-start = ((), (), s32[]{:S(2)}) async-start(), calls=%async_computation.4 | async-start | bytes 9175040 | tf_op jit(solution)/shard_map/all_gather | solution.py:17
  7.3 278.1 %all-gather.7.cloned.1.call-start = ((), (), s32[]{:S(2)}) async-start(), calls=%async_computation.6 | async-start | bytes 9175040 | tf_op jit(solution)/shard_map/all_gather | solution.py:18
  8.0 402.1 %reduce-scatter.4.cloned.1.call-start = ((), (), s32[]{:S(2)}) async-start(), calls=%async_computation.5 | async-start | bytes 4128768 | tf_op jit(solution)/shard_map/reduce_scatter | solution.py:20
  156.5 373.0 %reduce-scatter.6.cloned.1.call-start = ((), (), s32[]{:S(2)}) async-start(), calls=%async_computation.7 | async-start | bytes 4128768 | tf_op jit(solution)/shard_map/reduce_scatter | solution.py:23
  293.9 369.0 %all-gather.11.cloned.1.call-start = ((), (), s32[]{:S(2)}) async-start(), calls=%async_computation.9 | async-start | bytes 9175040 | tf_op jit(solution)/shard_map/all_gather | solution.py:31
  294.5 468.8 %all-gather.9.cloned.1.call-start = ((), (), s32[]{:S(2)}) async-start(), calls=%async_computation.8 | async-start | bytes 4128768 | tf_op jit(solution)/shard_map/all_gather | solution.py:28
  531.7 271.2 %reduce-scatter.8.cloned.1.call-start = ((), (), s32[]{:S(2)}) async-start(), calls=%async_computation.10 | async-start | bytes 1179648 | tf_op jit(solution)/shard_map/reduce_scatter | solution.py:34
Sparse Core Ops, SparseCore 0:
  9.2 138.7 all-gather.4
  149.8 135.5 all-gather.6
  289.6 120.4 reduce-scatter.3
  414.8 114.6 reduce-scatter.5
  531.1 131.6 all-gather.10
  665.3 97.9 all-gather.8
  772.6 30.3 reduce-scatter.7
